TPU v7x, 32 devices: a whole 2x2x4 slice. The times are simulated.
32 devices in a mesh: occ: 8 (over z, x), virt: 4 (over y, core).
Axes of the slice: x: 2, y: 2, z: 4, core: 2. Of those that a mesh axis runs over, the one named last changes fastest.
Arguments:
- factors: float32 [64, 512, 512], P('occ'), may hold values from -0.9 to 0.9
- occ_energy: float32 [64], replicated, may hold values from -3 to -0.5
- virt_energy: float32 [512], replicated, may hold values from 0.5 to 9.5
- pairing: int32 [2, 8], replicated, may hold values from 0 to 7, as said below
Outputs:
- pair_energy: float32 [2, 64], P(None, 'occ')
- gradient: float32 [64, 512, 512], P('occ', 'virt')
Inputs may be any that keep to these rules, and one draw needn't show every extreme that they name: `pairing`: in every round each group's partner is another group whose partner is that group.
All inputs are finite; a program needn't handle non-finite values.
Results may differ from a plain program's by a relative error of at most 0.0001.
Values sent between devices are 32-bit elements; how exact they have to be, the bound alone decides.
A program may use at most 192 MiB of HBM per device.

v0:
```python
import jax
import jax.numpy as jnp
from jax import lax
from jax.sharding import PartitionSpec as P

OG = 8
V = 512
ROUNDS = 2


def block_amplitude(
    own_rows, mate_rows, own_piece, fragment, own_energy, mate_energy, energy_left, energy_right
):
    highest = lax.Precision.HIGHEST
    groups_rows, slab_width, naux_width = own_rows.shape
    frag_width = fragment.shape[1]
    contract = (((1,), (1,)), ((), ()))
    coulomb = lax.dot_general(
        own_rows.reshape(groups_rows * slab_width, naux_width),
        fragment.reshape(groups_rows * frag_width, naux_width),
        contract,
        precision=highest,
        preferred_element_type=jnp.float32,
    )
    coulomb = coulomb.reshape(groups_rows, slab_width, groups_rows, frag_width)
    swapped = lax.dot_general(
        own_piece.reshape(groups_rows * frag_width, naux_width),
        mate_rows.reshape(groups_rows * slab_width, naux_width),
        contract,
        precision=highest,
        preferred_element_type=jnp.float32,
    )
    swapped = swapped.reshape(groups_rows, frag_width, groups_rows, slab_width).transpose(
        0, 3, 2, 1
    )
    denominator = (
        energy_left[None, :, None, None]
        + energy_right[None, None, None, :]
        - own_energy[:, None, None, None]
        - mate_energy[None, None, :, None]
    )
    amplitude = -(2.0 * coulomb - swapped) / denominator
    return (amplitude, coulomb)


def block_terms(
    own_rows, mate_rows, own_piece, fragment, own_energy, mate_energy, energy_left, energy_right
):
    highest = lax.Precision.HIGHEST
    groups_rows, slab_width, naux_width = own_rows.shape
    frag_width = fragment.shape[1]
    amplitude, coulomb = block_amplitude(
        own_rows, mate_rows, own_piece, fragment, own_energy, mate_energy, energy_left, energy_right
    )
    energy = jnp.sum(amplitude * coulomb, axis=(1, 2, 3))
    grad_part = jnp.dot(
        amplitude.reshape(groups_rows * slab_width, groups_rows * frag_width),
        fragment.reshape(groups_rows * frag_width, naux_width),
        precision=highest,
        preferred_element_type=jnp.float32,
    )
    return (energy, grad_part)


def route_slab(own_rows, partner_row, group_count):
    groups_rows, slab_width, naux_width = own_rows.shape
    split_rows = own_rows.reshape(group_count, groups_rows * slab_width // group_count, naux_width)
    mixed = lax.all_to_all(split_rows, "occ", split_axis=0, concat_axis=0, tiled=True)
    ordered = jnp.take(mixed, partner_row, axis=0)
    arrived = lax.all_to_all(ordered, "occ", split_axis=0, concat_axis=0, tiled=True)
    return arrived.reshape(groups_rows, slab_width, naux_width)


def per_device(factors, occ_energy, virt_energy, pairing):
    group_index = lax.axis_index("occ")
    column_index = lax.axis_index("virt")
    group_count = lax.axis_size("occ")
    virt_count = lax.axis_size("virt")
    groups_rows, virt_width, naux_width = factors.shape
    slab_width = virt_width // virt_count
    own_rows = lax.dynamic_slice_in_dim(factors, column_index * slab_width, slab_width, 1)
    own_energy = lax.dynamic_slice_in_dim(occ_energy, group_index * groups_rows, groups_rows, 0)
    energy_left = lax.dynamic_slice_in_dim(virt_energy, column_index * slab_width, slab_width, 0)
    total_grad = jnp.zeros((groups_rows * slab_width, naux_width), jnp.float32)
    energy_rows = []
    for round_index in range(ROUNDS):
        partner_row = pairing[round_index]
        mate_index = partner_row[group_index]
        mate_energy = lax.dynamic_slice_in_dim(occ_energy, mate_index * groups_rows, groups_rows, 0)
        partner_row, mate_energy = (partner_row, mate_energy)
        mate_rows = route_slab(own_rows, partner_row, group_count)

        def fold_step(carry, fragment, offset, mate_rows=mate_rows, mate_energy=mate_energy):
            own_piece, energy_right = (factors, virt_energy)
            energy, grad_part = block_terms(
                own_rows,
                mate_rows,
                own_piece,
                fragment,
                own_energy,
                mate_energy,
                energy_left,
                energy_right,
            )
            return (carry[0] + grad_part, energy)

        total_grad, energy_now = fold_step(
            (total_grad, jnp.zeros((groups_rows,), jnp.float32)),
            lax.all_gather(mate_rows, "virt", axis=1, tiled=True),
            jnp.int32(0),
        )
        energy_rows.append(energy_now)
    stacked = jnp.stack(energy_rows)
    stacked = stacked / (V * OG * V)
    pair_energy = lax.psum(stacked, "virt")
    return (pair_energy, total_grad.reshape(groups_rows, slab_width, naux_width))


def solution(mesh):
    placed = (P("occ", None, None), P(), P(), P())
    return jax.shard_map(
        per_device,
        mesh=mesh,
        in_specs=placed,
        out_specs=(P(None, "occ"), P("occ", "virt", None)),
        check_vma=False,
    )
```

profile of v0, /device:TPU:0, one launch (start us, length us, event | category | flops | bytes accessed | tf_op | source)
XLA Modules:
  0.0 512.6 jit_solution(10723391178314424963)
XLA Ops:
  7.2 0.0 copy-start.4
  7.2 3.1 constant_dynamic-slice_fusion.2
  10.2 7.3 %all-to-all-start = ((f32[8,128,512]{2,1,0:T(8,128)}), f32[8,128,512]{2,1,0:T(8,128)S(1)}, u32[]{:S(2)}, u32[]{:S(2)}) async-start(f32[8,128,512]{2,1,0:T(8,128)} %constant_dynamic-slice_fusion.2), calls=%async_computation | async-start | bytes 4194304 | tf_op jit(solution)/shard_map/all_to_all | solution.py:68
  17.5 0.0 all-gather.5.cloned.1.call-start
  17.6 0.0 copy-done.4
  17.6 48.2 %all-to-all-done = f32[8,128,512]{2,1,0:T(8,128)S(1)} async-done(((f32[8,128,512]{2,1,0:T(8,128)}), f32[8,128,512]{2,1,0:T(8,128)S(1)}, u32[]{:S(2)}, u32[]{:S(2)}) %all-to-all-start) | async-done | bytes 2097184 | tf_op jit(solution)/shard_map/all_to_all | solution.py:68
  65.8 2.0 gather_fusion.1
  67.8 1.9 broadcast_select_fusion
  69.7 51.9 %all_to_all.16 = f32[8,128,512]{2,1,0:T(8,128)} all-to-all(f32[8,128,512]{2,1,0:T(8,128)S(1)} %broadcast_select_fusion), channel_id=1, replica_groups=mesh['occ'=8,'virt'=4] {'occ'}, dimensions={0} | all-to-all | bytes 4194304 | tf_op jit(solution)/shard_map/all_to_all | solution.py:70
  121.6 0.0 all-gather.5.cloned.1.call-update
  121.6 0.0 all-gather.3.cloned.1.call-start
  121.7 2.0 gather_fusion
  123.7 1.9 broadcast_select_fusion.1
  125.6 51.5 %all_to_all.17 = f32[8,128,512]{2,1,0:T(8,128)} all-to-all(f32[8,128,512]{2,1,0:T(8,128)S(1)} %broadcast_select_fusion.1), channel_id=1, replica_groups=mesh['occ'=8,'virt'=4] {'occ'}, dimensions={0} | all-to-all | bytes 4194304 | tf_op jit(solution)/shard_map/all_to_all | solution.py:70
  177.1 0.0 all-gather.3.cloned.1.call-update
  177.1 0.6 fusion.14
  180.3 0.0 copy-done.5
  180.3 0.1 dynamic_slice.22
  181.7 0.0 copy-done.3
  181.7 0.1 fusion.13
  181.8 0.1 broadcast_add_fusion
  181.9 1.7 broadcast_subtract_fusion
  183.5 29.9 %fusion.16 = f32[1024,4096]{1,0:T(8,128)S(1)} fusion(f32[1024,512]{1,0:T(8,128)} %bitcast.82, f32[4096,512]{1,0:T(8,128)} %bitcast.77), kind=kOutput, calls=%fused_computation.35 | convolution fusion | flops 25769803776 | bytes 27262976 | tf_op jit(solution)/shard_map/dot_general | solution.py:26
  213.5 0.0 slice-start.1
  213.5 0.0 copy-start.1
  213.5 19.3 %copy.17 = f32[128,8,8,512]{3,2,1,0:T(8,128)} copy(f32[128,8,8,512]{3,1,2,0:T(8,128)S(1)} %bitcast.75) | data formatting | bytes 33554432
  232.8 0.0 slice-done
  232.8 0.0 slice-done.1
  232.9 0.0 copy-done.1
  232.9 27.8 %fusion.17 = f32[1024,4096]{1,0:T(8,128)S(1)} fusion(f32[1024,512]{1,0:T(8,128)S(1)} %bitcast.81, f32[4096,512]{1,0:T(8,128)S(1)} %bitcast.80), kind=kOutput, calls=%fused_computation.36 | convolution fusion | flops 25769803776 | bytes 27262976 | tf_op jit(solution)/shard_map/dot_general | solution.py:26
  260.7 0.0 copy-start
  260.7 19.5 %copy.18 = f32[128,8,8,512]{3,2,1,0:T(8,128)} copy(f32[128,8,8,512]{3,1,2,0:T(8,128)S(1)} %bitcast.76) | data formatting | bytes 33554432
  280.2 0.0 copy-done
  280.2 31.2 %fusion.4 = f32[8,128,8,512]{3,1,2,0:T(8,128)} fusion(f32[8,512,512]{2,1,0:T(8,128)} %all-gather.5.cloned.1.call-done, f32[8,128,512]{2,1,0:T(8,128)S(1)} %copy-done), kind=kOutput, calls=%fused_computation.10 | convolution fusion | flops 25769803776 | bytes 27262976 | tf_op jit(solution)/shard_map/dot_general | solution.py:18
  311.4 53.1 %multiply_reduce_fusion.1 = (f32[8]{0:T(128)S(1)}, f32[8,128,8,512]{3,1,2,0:T(8,128)}, f32[8]{0:T(128)S(1)}, f32[8,128,8,512]{3,1,2,0:T(8,128)}) fusion(f32[8]{0:T(128)S(1)} %get-tuple-element.17, f32[8,128,512]{2,1,0:T(8,128)} %broadcast_subtract_fusion, f32[8,512,8,128]{1,0,3,2:T(8,128)} %bitcast.83, f32[8,128,8,512]{3,1,2,0:T(8,128)} %fusion.4, ...), kind=kOutput, calls=%fused_computation.9 | convolution fusion | flops 25828524032 | bytes 96469120 | tf_op jit(solution)/shard_map/dot_general | solution.py:18
  364.5 6.4 %psum.7 = f32[2,8]{1,0:T(2,128)} all-reduce(f32[2,8]{1,0:T(2,128)S(1)} %maximum_multiply_fusion), channel_id=1, replica_groups=mesh['occ'=8,'virt'=4] {'virt'}, use_global_device_ids=true, to_apply=%region_2.4 | all-reduce | flops 16 | bytes 128 | tf_op jit(solution)/shard_map/psum | solution.py:115
  370.9 15.3 %copy.10 = f32[8,128,8,512]{3,2,1,0:T(8,128)S(1)} copy(f32[8,128,8,512]{3,1,2,0:T(8,128)} %get-tuple-element.4) | data formatting | bytes 33554432 | tf_op jit(solution)/shard_map/div | solution.py:42
  386.3 0.0 slice-start.4
  386.3 0.0 slice-start.5
  386.3 19.1 %copy.19 = f32[128,8,8,512]{3,1,2,0:T(8,128)} copy(f32[128,8,8,512]{3,2,1,0:T(8,128)S(1)} %bitcast.73) | data formatting | bytes 33554432
  405.5 0.0 slice-done.2
  405.5 0.0 slice-done.3
  405.5 0.0 slice-done.4
  405.5 0.0 slice-done.5
  405.5 20.1 %copy.11 = f32[8,128,8,512]{3,2,1,0:T(8,128)S(1)} copy(f32[8,128,8,512]{3,1,2,0:T(8,128)S(1)} %bitcast.86) | data formatting | bytes 33554432 | tf_op jit(solution)/shard_map/div | solution.py:42
  425.7 19.5 %copy.20 = f32[128,8,8,512]{3,1,2,0:T(8,128)} copy(f32[128,8,8,512]{3,2,1,0:T(8,128)S(1)} %bitcast.74) | data formatting | bytes 33554432
  445.1 28.6 %fusion.18 = f32[1024,512]{1,0:T(8,128)S(1)} fusion(f32[1024,4096]{1,0:T(8,128)S(1)} %bitcast.87, f32[4096,512]{1,0:T(8,128)} %bitcast.92), kind=kOutput, calls=%fused_computation.37 | convolution fusion | flops 25769803776 | bytes 27262976 | tf_op jit(solution)/shard_map/dot_general | solution.py:56
  473.7 31.5 %convolution_add_fusion = f32[1024,512]{1,0:T(8,128)} fusion(f32[1024,512]{1,0:T(8,128)S(1)} %fusion.18, f32[1024,4096]{1,0:T(8,128)} %bitcast.88, f32[4096,512]{1,0:T(8,128)} %bitcast.89), kind=kOutput, calls=%fused_computation.16 | convolution fusion | flops 25770328064 | bytes 29360128 | tf_op jit(solution)/shard_map/dot_general | solution.py:56
  (16 shorter events, 0.1 us)
Async XLA Ops:
  7.2 10.4 %copy-start.4 = (s32[2,8]{1,0:T(2,128)S(1)}, s32[2,8]{1,0:T(2,128)}, u32[]{:S(2)}) copy-start(s32[2,8]{1,0:T(2,128)} %param.9) | copy-start | bytes 196
  10.2 55.5 %all-to-all-start = ((f32[8,128,512]{2,1,0:T(8,128)}), f32[8,128,512]{2,1,0:T(8,128)S(1)}, u32[]{:S(2)}, u32[]{:S(2)}) async-start(f32[8,128,512]{2,1,0:T(8,128)} %constant_dynamic-slice_fusion.2), calls=%async_computation | async-start | bytes 4194304 | tf_op jit(solution)/shard_map/all_to_all | solution.py:68
  17.5 262.6 %all-gather.5.cloned.1.call-start = ((), (), s32[]{:S(2)}) async-start(), calls=%async_computation.4 | async-start | bytes 10485760 | tf_op jit(solution)/shard_map/all_gather | solution.py:109
  121.6 58.7 %copy-start.5 = (f32[512]{0:T(512)S(1)}, f32[512]{0:T(512)}, u32[]{:S(2)}) copy-start(f32[512]{0:T(512)} %param.8) | copy-start | bytes 6148
  121.6 60.1 %copy-start.3 = (f32[64]{0:T(128)S(1)}, f32[64]{0:T(128)}, u32[]{:S(2)}) copy-start(f32[64]{0:T(128)} %param.7) | copy-start | bytes 772
  121.6 189.8 %all-gather.3.cloned.1.call-start = ((), (), s32[]{:S(2)}) async-start(), calls=%async_computation.3 | async-start | bytes 10485760 | tf_op jit(solution)/shard_map/all_gather | solution.py:109
  183.5 49.3 %slice-start = ((s8[8388608]{0:T(1024)(128)(4,1)}), s8[4194304]{0:T(1024)(128)(4,1)S(1)}, s32[]{:S(2)}) async-start(s8[8388608]{0:T(1024)(128)(4,1)} %bitcast.78), calls=%async_computation.5 | async-start | bytes 8388608
  213.5 19.4 %slice-start.1 = ((s8[8388608]{0:T(1024)(128)(4,1)}), s8[4194304]{0:T(1024)(128)(4,1)S(1)}, s32[]{:S(2)}) async-start(s8[8388608]{0:T(1024)(128)(4,1)} %bitcast.78), calls=%async_computation.6 | async-start | bytes 8388608
  213.5 19.4 %copy-start.1 = (f32[8,128,512]{2,1,0:T(8,128)S(1)}, f32[8,128,512]{2,1,0:T(8,128)}, u32[]{:S(2)}) copy-start(f32[8,128,512]{2,1,0:T(8,128)} %all_to_all.16) | copy-start | bytes 6291460
  260.7 19.5 %copy-start = (f32[8,128,512]{2,1,0:T(8,128)S(1)}, f32[8,128,512]{2,1,0:T(8,128)}, u32[]{:S(2)}) copy-start(f32[8,128,512]{2,1,0:T(8,128)} %constant_dynamic-slice_fusion.2) | copy-start | bytes 6291460
  370.9 34.5 %slice-start.2 = ((s8[16777216]{0:T(1024)(128)(4,1)}), s8[4194304]{0:T(1024)(128)(4,1)S(1)}, s32[]{:S(2)}) async-start(s8[16777216]{0:T(1024)(128)(4,1)} %bitcast.85), calls=%async_computation.7 | async-start | bytes 8388608
  370.9 34.5 %slice-start.3 = ((s8[16777216]{0:T(1024)(128)(4,1)}), s8[4194304]{0:T(1024)(128)(4,1)S(1)}, s32[]{:S(2)}) async-start(s8[16777216]{0:T(1024)(128)(4,1)} %bitcast.85), calls=%async_computation.8 | async-start | bytes 8388608
  386.3 19.2 %slice-start.4 = ((s8[16777216]{0:T(1024)(128)(4,1)}), s8[4194304]{0:T(1024)(128)(4,1)S(1)}, s32[]{:S(2)}) async-start(s8[16777216]{0:T(1024)(128)(4,1)} %bitcast.85), calls=%async_computation.9 | async-start | bytes 8388608
  386.3 19.2 %slice-start.5 = ((s8[16777216]{0:T(1024)(128)(4,1)}), s8[4194304]{0:T(1024)(128)(4,1)S(1)}, s32[]{:S(2)}) async-start(s8[16777216]{0:T(1024)(128)(4,1)} %bitcast.85), calls=%async_computation.10 | async-start | bytes 8388608
  425.6 19.5 %copy-start.2 = (f32[128,8,8,512]{3,1,2,0:T(8,128)S(1)}, f32[128,8,8,512]{3,1,2,0:T(8,128)}, u32[]{:S(2)}) copy-start(f32[128,8,8,512]{3,1,2,0:T(8,128)} %copy.19) | copy-start | bytes 50331652
Sparse Core Ops, SparseCore 0:
  121.7 57.3 all-gather.4
  180.7 58.2 all-gather.2
where the time goes:
time: 523 us; the launch traced here: 513 us
  matrix products  202 us (39%)
  local copies, waits for them, and re-layouts  120 us (23%)
  blocking collectives  110 us (21%)
  waiting for transfers between devices  48.2 us (9%)
  between operations  18.7 us (4%)
  starting transfers between devices  7.36 us (1%)
  other arithmetic  6.14 us (1%)
    all_to_all x2, blocking collectives, route_slab(): lax.all_to_all(ordered, 'occ', split_axis=0, concat_axis=0, tiled=True)  103 us
    dot_general x2, matrix products, block_amplitude(): lax.dot_general(own_rows.reshape(groups_rows * slab_width, naux_width), f...  84.3 us
    unnamed x28, local copies, waits for them, and re-layouts  77.5 us
    dot_general x2, matrix products, block_terms(): jnp.dot(amplitude.reshape(groups_rows * slab_width, groups_rows * frag_wi...  60.1 us
    dot_general x2, matrix products, block_amplitude(): lax.dot_general(own_piece.reshape(groups_rows * frag_width, naux_width),...  57.8 us
    all_to_all x1, waiting for transfers between devices, route_slab(): lax.all_to_all(split_rows, 'occ', split_axis=0, concat_axis=0, tiled=True)  48.2 us
    div x2, local copies, waits for them, and re-layouts, block_amplitude(): amplitude = -(2.0 * coulomb - swapped) / denominator  35.5 us
  transfers between devices with their start and end apart: 3, of which 1 were waited for; matrix products, arithmetic and copies ran while one was open for 26% of the time, Pallas kernels for 0%

commit v1 on v0

--- a/solution.py
+++ b/solution.py
@@ -1,6 +1,10 @@
+import functools
+
 import jax
 import jax.numpy as jnp
 from jax import lax
+from jax.experimental import pallas as pl
+from jax.experimental.pallas import tpu as pltpu
 from jax.sharding import PartitionSpec as P
 
 OG = 8
@@ -71,7 +75,7 @@
     return arrived.reshape(groups_rows, slab_width, naux_width)
 
 
-def per_device(factors, occ_energy, virt_energy, pairing):
+def per_device_slabs(factors, occ_energy, virt_energy, pairing):
     group_index = lax.axis_index("occ")
     column_index = lax.axis_index("virt")
     group_count = lax.axis_size("occ")
@@ -116,6 +120,164 @@
     return (pair_energy, total_grad.reshape(groups_rows, slab_width, naux_width))
 
 
+CHUNKS = 4
+
+
+def split_hi_lo(values):
+    high = values.astype(jnp.bfloat16)
+    low = (values - high.astype(jnp.float32)).astype(jnp.bfloat16)
+    return high, low
+
+
+def pair_kernel(
+    mate_count,
+    pairing_ref,
+    occ_ref,
+    own_ref,
+    mates_ref,
+    left_ref,
+    right_ref,
+    grad_ref,
+    energy_ref,
+    own_wide,
+    mate_wide,
+    mate_tall,
+    amp_wide,
+    total,
+):
+    row, step = pl.program_id(0), pl.program_id(1)
+    steps = pl.num_programs(1)
+    virt_width, naux_width = total.shape
+    depth = naux_width
+
+    @pl.when(row == 0)
+    def _():
+        high, low = split_hi_lo(mates_ref[0, 0])
+        mate_wide[step, :, :depth] = high
+        mate_wide[step, :, depth : 2 * depth] = high
+        mate_wide[step, :, 2 * depth :] = low
+        mate_tall[step, :virt_width] = high
+        mate_tall[step, virt_width : 2 * virt_width] = high
+        mate_tall[step, 2 * virt_width :] = low
+
+    @pl.when(step == 0)
+    def _():
+        high, low = split_hi_lo(own_ref[0])
+        own_wide[:, :depth] = high
+        own_wide[:, depth : 2 * depth] = low
+        own_wide[:, 2 * depth :] = high
+
+    coulomb = lax.dot_general(
+        own_wide[...],
+        mate_wide[step],
+        (((1,), (1,)), ((), ())),
+        preferred_element_type=jnp.float32,
+    )
+    round_index, mate = step // mate_count, step % mate_count
+    own_energy = occ_ref[0, row]
+    mate_energy = occ_ref[1 + round_index, mate]
+    denominator = left_ref[...] + right_ref[...] - own_energy - mate_energy
+    amplitude = (coulomb.T - 2.0 * coulomb) / denominator
+    energy_ref[0, 0] = (amplitude * coulomb).reshape(virt_width // 8, 8, virt_width).sum(0)
+    high, low = split_hi_lo(amplitude)
+    amp_wide[:, :virt_width] = high
+    amp_wide[:, virt_width : 2 * virt_width] = low
+    amp_wide[:, 2 * virt_width :] = high
+    part = jnp.dot(amp_wide[...], mate_tall[step], preferred_element_type=jnp.float32)
+
+    @pl.when(step == 0)
+    def _():
+        total[...] = part
+
+    @pl.when(step > 0)
+    def _():
+        total[...] += part
+
+    @pl.when(step == steps - 1)
+    def _():
+        grad_ref[0] = total[...]
+
+
+def pair_rows(own, first, rows, mates, partners, energies, virt_energy):
+    _, virt_width, naux_width = own.shape
+    mate_count = mates.shape[1]
+    rounds = partners.shape[0]
+    steps = rounds * mate_count
+
+    def mate_map(row, step, partners_ref, energies_ref):
+        now = jnp.where(row == 0, step, steps - 1)
+        return partners_ref[now // mate_count], now % mate_count, 0, 0
+
+    flops = 2 * 2 * 3 * rows * steps * virt_width * virt_width * naux_width
+    return pl.pallas_call(
+        functools.partial(pair_kernel, mate_count),
+        grid_spec=pltpu.PrefetchScalarGridSpec(
+            num_scalar_prefetch=2,
+            grid=(rows, steps),
+            in_specs=[
+                pl.BlockSpec((1, virt_width, naux_width), lambda i, s, p, e: (first + i, 0, 0)),
+                pl.BlockSpec((1, 1, virt_width, naux_width), mate_map),
+                pl.BlockSpec((virt_width, 1), lambda i, s, p, e: (0, 0)),
+                pl.BlockSpec((1, virt_width), lambda i, s, p, e: (0, 0)),
+            ],
+            out_specs=[
+                pl.BlockSpec((1, virt_width, naux_width), lambda i, s, p, e: (i, 0, 0)),
+                pl.BlockSpec((1, 1, 8, virt_width), lambda i, s, p, e: (i, s, 0, 0)),
+            ],
+            scratch_shapes=[
+                pltpu.VMEM((virt_width, 3 * naux_width), jnp.bfloat16),
+                pltpu.VMEM((steps, virt_width, 3 * naux_width), jnp.bfloat16),
+                pltpu.VMEM((steps, 3 * virt_width, naux_width), jnp.bfloat16),
+                pltpu.VMEM((virt_width, 3 * virt_width), jnp.bfloat16),
+                pltpu.VMEM((virt_width, naux_width), jnp.float32),
+            ],
+        ),
+        out_shape=[
+            jax.ShapeDtypeStruct((rows, virt_width, naux_width), jnp.float32),
+            jax.ShapeDtypeStruct((rows, steps, 8, virt_width), jnp.float32),
+        ],
+        cost_estimate=pl.CostEstimate(flops=flops, bytes_accessed=2**24, transcendentals=0),
+        name="pair_rows",
+    )(partners, energies, own, mates, virt_energy[:, None], virt_energy[None, :])
+
+
+def spread_mates(share):
+    return lax.all_gather(share, "occ", axis=0, tiled=False)
+
+
+def per_device(factors, occ_energy, virt_energy, pairing):
+    group_index = lax.axis_index("occ")
+    column_index = lax.axis_index("virt")
+    virt_count = lax.axis_size("virt")
+    groups_rows, virt_width, naux_width = factors.shape
+    if groups_rows % virt_count or groups_rows % CHUNKS:
+        return per_device_slabs(factors, occ_energy, virt_energy, pairing)
+    mate_count = groups_rows // virt_count
+    rounds = pairing.shape[0]
+    share = lax.dynamic_slice_in_dim(factors, column_index * mate_count, mate_count, 0)
+    mates = spread_mates(share)
+    partners = pairing[:, group_index]
+    grouped = occ_energy.reshape(-1, groups_rows)
+    own_energy = grouped[group_index]
+    mate_energy = lax.dynamic_slice_in_dim(
+        grouped[partners], column_index * mate_count, mate_count, 1
+    )
+    rows = groups_rows // CHUNKS
+    width = max(rows, mate_count)
+    mate_energy = jnp.pad(mate_energy, ((0, 0), (0, width - mate_count)))
+    energy_parts, grads = [], []
+    for chunk in range(CHUNKS):
+        picked = slice(chunk * rows, (chunk + 1) * rows)
+        energies = jnp.pad(own_energy[None, picked], ((0, 0), (0, width - rows)))
+        energies = jnp.concatenate([energies, mate_energy])
+        grad, energy = pair_rows(factors, chunk * rows, rows, mates, partners, energies, virt_energy)
+        grads.append(lax.psum_scatter(grad, "virt", scatter_dimension=1, tiled=True))
+        energy = energy.reshape(rows, rounds, -1).sum(2).T
+        energy_parts.append(energy)
+    stacked = jnp.concatenate(energy_parts, axis=1) / (virt_width * groups_rows * virt_width)
+    return lax.psum(stacked, "virt"), jnp.concatenate(grads, axis=0)
+
+
 def solution(mesh):
     placed = (P("occ", None, None), P(), P(), P())
     return jax.shard_map(

time: 523 us -> 404 us (0.77); the launches traced: 513 us -> 403 us
  waiting for transfers between devices: 48.2 us -> 283 us
  matrix products: 202 us -> 0 us
  local copies, waits for them, and re-layouts: 120 us -> 6.89 us
  blocking collectives: 110 us -> 6.44 us
  Pallas kernels: 0 us -> 87.5 us
  starting transfers between devices: 7.36 us -> 0.21 us
    all_gather x2 -> x1, waiting for transfers between devices: 0.01 us -> 227 us  [spread_mates(): return lax.all_gather(share, 'occ', axis=0, tiled=False)]
    dot_general x6 -> x0, matrix products: 202 us -> none  [the longest x2 84.3 us: block_amplitude(): lax.dot_general(own_rows.reshape(groups_rows * slab_width, naux_width), f...]
    all_to_all x2 -> x0, blocking collectives: 103 us -> none  [route_slab(): lax.all_to_all(ordered, 'occ', split_axis=0, concat_axis=0, tiled=True)]
    pallas_call x0 -> x4, Pallas kernels: none -> 87.5 us  [pair_rows(): pl.pallas_call(functools.partial(pair_kernel, mate_count), grid_spec=pltp...]
    unnamed x28 -> x14, local copies, waits for them, and re-layouts: 77.5 us -> 1.44 us
    reduce_scatter x0 -> x4, waiting for transfers between devices: none -> 56.3 us  [per_device(): lax.psum_scatter(grad, 'virt', scatter_dimension=1, tiled=True)]
    all_to_all x1 -> x0, waiting for transfers between devices: 48.2 us -> none  [route_slab(): lax.all_to_all(split_rows, 'occ', split_axis=0, concat_axis=0, tiled=True)]
    div x2 -> x0, local copies, waits for them, and re-layouts: 35.5 us -> none  [block_amplitude(): amplitude = -(2.0 * coulomb - swapped) / denominator]
  transfers between devices with their start and end apart: 3 -> 5, of which waited for: 1 -> 3; matrix products, arithmetic and copies ran while one was open for 26% -> 1% of each run, Pallas kernels for 0% -> 16%
where the time goes in v1:
time: 404 us; the launch traced here: 403 us
  waiting for transfers between devices  283 us (70%)
  Pallas kernels  87.5 us (22%)
  between operations  13.8 us (3%)
  local copies, waits for them, and re-layouts  6.89 us (2%)
  blocking collectives  6.44 us (2%)
  other arithmetic  5.24 us (1%)
    all_gather x1, waiting for transfers between devices, spread_mates(): return lax.all_gather(share, 'occ', axis=0, tiled=False)  227 us
    pallas_call x4, Pallas kernels, pair_rows(): pl.pallas_call(functools.partial(pair_kernel, mate_count), grid_spec=pltp...  87.5 us
    reduce_scatter x4, waiting for transfers between devices, per_device(): lax.psum_scatter(grad, 'virt', scatter_dimension=1, tiled=True)  56.3 us
  transfers between devices with their start and end apart: 5, of which 3 were waited for; matrix products, arithmetic and copies ran while one was open for 1% of the time, Pallas kernels for 16%

profile of v1, /device:TPU:0, one launch (start us, length us, event | category | flops | bytes accessed | tf_op | source)
XLA Modules:
  0.0 403.2 jit_solution(5528561191939919819)
XLA Ops:
  7.2 0.0 all-gather.3.cloned.1.call-start
  7.2 3.1 constant_dynamic-slice_fusion
  10.3 0.0 all-gather.3.cloned.1.call-update
  10.3 0.0 reduce-scatter.5.cloned.1.call-start
  10.4 0.6 copy-done.6
  11.0 0.1 reshape.23
  11.0 0.0 copy-done.4
  11.0 0.9 copy.15.left_ref
  11.9 0.0 copy-done.5
  11.9 0.7 fusion
  12.6 0.6 gather_fusion
  13.2 0.1 constant_dynamic-slice_fusion.1
  13.2 0.1 fusion.2
  13.3 0.6 pad_maximum_fusion.4
  13.9 226.8 %all-gather.3.cloned.1.call-done = f32[16,512,512]{2,1,0:T(8,128)} async-done(((f32[2,512,512]{2,1,0:T(8,128)}), f32[16,512,512]{2,1,0:T(8,128)}) %all-gather.3.cloned.1.call-update) | async-done | bytes 16777232 | tf_op jit(solution)/shard_map/all_gather | solution.py:245
  240.7 21.9 %pair_rows.4 = (f32[2,512,512]{2,1,0:T(8,128)}, f32[2,4,8,512]{3,2,1,0:T(8,128)}) custom-call(s32[2]{0:T(128)} %get-tuple-element.21.pairing_ref, f32[3,2]{1,0:T(4,128)} %get-tuple-element.22.occ_ref, f32[8,512,512]{2,1,0:T(8,128)} %own_ref.7, f32[8,2,512,512]{3,2,1,0:T(8,128)} %bitcast.16, f32[512,1]{1,0:T(8,128)} %copy.15.left_ref, f32[1,512]{1,0:T(1,128)} %bitcast.11), custom_call_target="tpu_custom_call" | custom-call | flops 12884901888 | bytes 16777216 | tf_op jit(solution)/shard_map/pair_rows/pallas_call | solution.py:212
  262.6 0.0 reduce-scatter.5.cloned.1.call-update
  262.6 0.0 reduce-scatter.7.cloned.1.call-start
  262.7 21.9 %pair_rows.5 = (f32[2,512,512]{2,1,0:T(8,128)}, f32[2,4,8,512]{3,2,1,0:T(8,128)}) custom-call(s32[2]{0:T(128)} %get-tuple-element.21.pairing_ref, f32[3,2]{1,0:T(4,128)} %get-tuple-element.23.occ_ref, f32[8,512,512]{2,1,0:T(8,128)} %own_ref.7, f32[8,2,512,512]{3,2,1,0:T(8,128)} %bitcast.17, f32[512,1]{1,0:T(8,128)} %copy.15.left_ref, f32[1,512]{1,0:T(1,128)} %bitcast.12), custom_call_target="tpu_custom_call" | custom-call | flops 12884901888 | bytes 16777216 | tf_op jit(solution)/shard_map/pair_rows/pallas_call | solution.py:212
  284.5 0.0 reduce-scatter.7.cloned.1.call-update
  284.5 0.0 reduce-scatter.9.cloned.1.call-start
  284.6 21.9 %pair_rows.6 = (f32[2,512,512]{2,1,0:T(8,128)}, f32[2,4,8,512]{3,2,1,0:T(8,128)}) custom-call(s32[2]{0:T(128)} %get-tuple-element.21.pairing_ref, f32[3,2]{1,0:T(4,128)} %get-tuple-element.24.occ_ref, f32[8,512,512]{2,1,0:T(8,128)} %own_ref.7, f32[8,2,512,512]{3,2,1,0:T(8,128)} %bitcast.18, f32[512,1]{1,0:T(8,128)} %copy.15.left_ref, f32[1,512]{1,0:T(1,128)} %bitcast.13), custom_call_target="tpu_custom_call" | custom-call | flops 12884901888 | bytes 16777216 | tf_op jit(solution)/shard_map/pair_rows/pallas_call | solution.py:212
  306.5 0.0 reduce-scatter.9.cloned.1.call-update
  306.5 0.0 reduce-scatter.11.cloned.1.call-start
  306.6 21.9 %pair_rows.7 = (f32[2,512,512]{2,1,0:T(8,128)}, f32[2,4,8,512]{3,2,1,0:T(8,128)}) custom-call(s32[2]{0:T(128)} %get-tuple-element.21.pairing_ref, f32[3,2]{1,0:T(4,128)} %get-tuple-element.25.occ_ref, f32[8,512,512]{2,1,0:T(8,128)} %own_ref.7, f32[8,2,512,512]{3,2,1,0:T(8,128)} %bitcast.19, f32[512,1]{1,0:T(8,128)} %copy.15.left_ref, f32[1,512]{1,0:T(1,128)} %bitcast.14), custom_call_target="tpu_custom_call" | custom-call | flops 12884901888 | bytes 16777216 | tf_op jit(solution)/shard_map/pair_rows/pallas_call | solution.py:212
  328.4 0.0 reduce-scatter.11.cloned.1.call-update
  328.5 0.9 copy-done
  329.3 0.1 reduce_sum.46
  329.4 0.1 reduce_sum.47
  329.5 0.1 reduce_sum.51
  329.6 0.1 copy.19
  329.7 0.1 reduce_sum.52
  329.8 0.1 reduce_sum.53
  329.9 0.1 reduce_sum.54
  330.0 0.1 copy.20
  330.1 0.1 reduce_sum.55
  330.2 0.1 reduce_sum.59
  330.3 0.1 reduce_sum.72
  330.4 0.1 copy.21
  330.5 0.1 reduce_sum.73
  330.6 0.1 reduce_sum.74
  330.7 0.1 reduce_sum.75
  330.8 0.1 copy.22
  330.9 0.1 maximum_multiply_fusion
  331.0 6.4 %psum.7 = f32[2,8]{1,0:T(2,128)} all-reduce(f32[2,8]{1,0:T(2,128)S(1)} %maximum_multiply_fusion), channel_id=1, replica_groups=mesh['occ'=8,'virt'=4] {'virt'}, use_global_device_ids=true, to_apply=%region_8.9 | all-reduce | flops 16 | bytes 128 | tf_op jit(solution)/shard_map/psum | solution.py:278
  337.4 22.1 %reduce-scatter.9.cloned.1.call-done = f32[2,128,512]{2,1,0:T(8,128)} async-done(((f32[2,512,512]{2,1,0:T(8,128)}), f32[2,128,512]{2,1,0:T(8,128)}) %reduce-scatter.9.cloned.1.call-update) | async-done | bytes 524304 | tf_op jit(solution)/shard_map/reduce_scatter | solution.py:274
  359.5 34.2 %reduce-scatter.11.cloned.1.call-done = f32[2,128,512]{2,1,0:T(8,128)} async-done(((f32[2,512,512]{2,1,0:T(8,128)}), f32[2,128,512]{2,1,0:T(8,128)}) %reduce-scatter.11.cloned.1.call-update) | async-done | bytes 524304 | tf_op jit(solution)/shard_map/reduce_scatter | solution.py:274
  393.7 3.0 pad_maximum_fusion
  (14 shorter events, 0.0 us)
Async XLA Ops:
  7.2 233.6 %all-gather.3.cloned.1.call-start = ((), (), s32[]{:S(2)}) async-start(), calls=%async_computation.8 | async-start | bytes 18874368 | tf_op jit(solution)/shard_map/all_gather | solution.py:245
  10.3 0.7 copy-start.6
  10.3 0.7 copy-start.4
  10.3 1.6 copy-start.5
  10.3 327.1 %reduce-scatter.5.cloned.1.call-start = ((), (), s32[]{:S(2)}) async-start(), calls=%async_computation.4 | async-start | bytes 2621440 | tf_op jit(solution)/shard_map/reduce_scatter | solution.py:274
  262.6 74.8 %reduce-scatter.7.cloned.1.call-start = ((), (), s32[]{:S(2)}) async-start(), calls=%async_computation.5 | async-start | bytes 2621440 | tf_op jit(solution)/shard_map/reduce_scatter | solution.py:274
  284.5 75.0 %reduce-scatter.9.cloned.1.call-start = ((), (), s32[]{:S(2)}) async-start(), calls=%async_computation.6 | async-start | bytes 2621440 | tf_op jit(solution)/shard_map/reduce_scatter | solution.py:274
  306.5 87.2 %reduce-scatter.11.cloned.1.call-start = ((), (), s32[]{:S(2)}) async-start(), calls=%async_computation.7 | async-start | bytes 2621440 | tf_op jit(solution)/shard_map/reduce_scatter | solution.py:274
  328.4 0.9 copy-start
  328.4 1.3 copy-start.1
  328.4 1.7 copy-start.2
  328.4 2.1 copy-start.3
Sparse Core Ops, SparseCore 0:
  10.7 229.9 all-gather.2
  262.7 29.3 reduce-scatter.4
  294.6 31.1 reduce-scatter.6
  328.3 31.2 reduce-scatter.8
  362.5 31.1 reduce-scatter.10

commit v2 on v0

--- a/solution.py
+++ b/solution.py
@@ -1,6 +1,10 @@
+import functools
+
 import jax
 import jax.numpy as jnp
 from jax import lax
+from jax.experimental import pallas as pl
+from jax.experimental.pallas import tpu as pltpu
 from jax.sharding import PartitionSpec as P
 
 OG = 8
@@ -71,7 +75,7 @@
     return arrived.reshape(groups_rows, slab_width, naux_width)
 
 
-def per_device(factors, occ_energy, virt_energy, pairing):
+def per_device_slabs(factors, occ_energy, virt_energy, pairing):
     group_index = lax.axis_index("occ")
     column_index = lax.axis_index("virt")
     group_count = lax.axis_size("occ")
@@ -116,8 +120,231 @@
     return (pair_energy, total_grad.reshape(groups_rows, slab_width, naux_width))
 
 
+CORES = 2
+
+
+def split_hi_lo(values):
+    high = values.astype(jnp.bfloat16)
+    low = (values - high.astype(jnp.float32)).astype(jnp.bfloat16)
+    return high, low
+
+
+def pair_kernel(half, energies_ref, own_ref, near_ref, far_ref, left_ref, right_ref, *rest):
+    carried_ref = rest[0] if len(rest) == 8 else None
+    grad_ref, energy_ref, own_wide, mate_wide, mate_tall, amp_wide, total = rest[-7:]
+    row, step = pl.program_id(0), pl.program_id(1)
+    steps = pl.num_programs(1)
+    virt_width, naux_width = total.shape
+    depth = naux_width
+
+    def hold_mate(mate):
+        high, low = split_hi_lo(mate)
+        mate_wide[step, :, :depth] = high
+        mate_wide[step, :, depth : 2 * depth] = high
+        mate_wide[step, :, 2 * depth :] = low
+        mate_tall[step, :virt_width] = high
+        mate_tall[step, virt_width : 2 * virt_width] = high
+        mate_tall[step, 2 * virt_width :] = low
+
+    @pl.when((row == 0) & (step < half))
+    def _():
+        hold_mate(near_ref[0])
+
+    @pl.when((row == 0) & (step >= half))
+    def _():
+        hold_mate(far_ref[0])
+
+    @pl.when(step == 0)
+    def _():
+        high, low = split_hi_lo(own_ref[0])
+        own_wide[:, :depth] = high
+        own_wide[:, depth : 2 * depth] = low
+        own_wide[:, 2 * depth :] = high
+        if carried_ref is None:
+            total[...] = jnp.zeros_like(total)
+        else:
+            total[...] = carried_ref[0]
+
+    coulomb = lax.dot_general(
+        own_wide[...],
+        mate_wide[step],
+        (((1,), (1,)), ((), ())),
+        preferred_element_type=jnp.float32,
+    )
+    own_energy = energies_ref[0, row]
+    mate_energy = energies_ref[1, step]
+    denominator = left_ref[...] + right_ref[...] - own_energy - mate_energy
+    amplitude = (coulomb.T - 2.0 * coulomb) / denominator
+    energy_ref[0, 0] = (amplitude * coulomb).reshape(virt_width // 8, 8, virt_width).sum(0)
+    high, low = split_hi_lo(amplitude)
+    amp_wide[:, :virt_width] = high
+    amp_wide[:, virt_width : 2 * virt_width] = low
+    amp_wide[:, 2 * virt_width :] = high
+    total[...] += jnp.dot(amp_wide[...], mate_tall[step], preferred_element_type=jnp.float32)
+
+    @pl.when(step == steps - 1)
+    def _():
+        grad_ref[0] = total[...]
+
+
+def pair_rows(own, first, rows, near, far, own_energy, mate_energy, virt_energy, carried):
+    _, virt_width, naux_width = own.shape
+    half = near.shape[0]
+    steps = 2 * half
+    width = max(rows, steps)
+    energies = jnp.stack(
+        [
+            jnp.pad(own_energy[first : first + rows], (0, width - rows)),
+            jnp.pad(mate_energy, (0, width - steps)),
+        ]
+    )
+    block = (1, virt_width, naux_width)
+
+    def near_map(i, s, e):
+        return jnp.where(i == 0, jnp.minimum(s, half - 1), half - 1), 0, 0
+
+    def far_map(i, s, e):
+        return jnp.where(i == 0, jnp.maximum(s - half, 0), half - 1), 0, 0
+
+    def own_map(i, s, e):
+        return first + i, 0, 0
+
+    in_specs = [
+        pl.BlockSpec(block, own_map),
+        pl.BlockSpec(block, near_map),
+        pl.BlockSpec(block, far_map),
+        pl.BlockSpec((virt_width, 1), lambda i, s, e: (0, 0)),
+        pl.BlockSpec((1, virt_width), lambda i, s, e: (0, 0)),
+    ]
+    operands = [own, near, far, virt_energy[:, None], virt_energy[None, :]]
+    if carried is not None:
+        in_specs.append(pl.BlockSpec(block, own_map))
+        operands.append(carried)
+    flops = 2 * 2 * 3 * rows * steps * virt_width * virt_width * naux_width
+    grad, energy = pl.pallas_call(
+        functools.partial(pair_kernel, half),
+        grid_spec=pltpu.PrefetchScalarGridSpec(
+            num_scalar_prefetch=1,
+            grid=(rows, steps),
+            in_specs=in_specs,
+            out_specs=[
+                pl.BlockSpec(block, lambda i, s, e: (i, 0, 0)),
+                pl.BlockSpec((1, 1, 8, virt_width), lambda i, s, e: (i, s, 0, 0)),
+            ],
+            scratch_shapes=[
+                pltpu.VMEM((virt_width, 3 * naux_width), jnp.bfloat16),
+                pltpu.VMEM((steps, virt_width, 3 * naux_width), jnp.bfloat16),
+                pltpu.VMEM((steps, 3 * virt_width, naux_width), jnp.bfloat16),
+                pltpu.VMEM((virt_width, 3 * virt_width), jnp.bfloat16),
+                pltpu.VMEM((virt_width, naux_width), jnp.float32),
+            ],
+        ),
+        out_shape=[
+            jax.ShapeDtypeStruct((rows, virt_width, naux_width), jnp.float32),
+            jax.ShapeDtypeStruct((rows, steps, 8, virt_width), jnp.float32),
+        ],
+        cost_estimate=pl.CostEstimate(flops=flops, bytes_accessed=2**24, transcendentals=0),
+        name="pair_rows",
+    )(energies, *operands)
+    return grad, energy.sum((1, 2, 3))
+
+
+def exchange_pieces(pieces, group_index, group_count):
+    arrived = lax.dynamic_update_index_in_dim(
+        jnp.zeros_like(pieces), lax.dynamic_index_in_dim(pieces, group_index, 0), group_index, 0
+    )
+    for shift in range(1, group_count):
+        sent = lax.dynamic_index_in_dim(pieces, lax.rem(group_index + shift, group_count), 0)
+        got = lax.ppermute(
+            sent, "occ", [(s, (s + shift) % group_count) for s in range(group_count)]
+        )
+        source = lax.rem(group_index + group_count - shift, group_count)
+        arrived = lax.dynamic_update_index_in_dim(arrived, got, source, 0)
+    return arrived
+
+
+def per_device(factors, occ_energy, virt_energy, pairing):
+    group_index = lax.axis_index("occ")
+    column_index = lax.axis_index("virt")
+    group_count = lax.axis_size("occ")
+    virt_count = lax.axis_size("virt")
+    groups_rows, virt_width, naux_width = factors.shape
+    if groups_rows % virt_count or virt_count % CORES or pairing.shape[0] != 2:
+        return per_device_slabs(factors, occ_energy, virt_energy, pairing)
+    span = virt_count // CORES
+    place, core = column_index // CORES, column_index % CORES
+    half = groups_rows // virt_count
+    own_count = groups_rows // CORES
+    slab = virt_width // virt_count
+    twin = [(v, v ^ 1) for v in range(virt_count)]
+
+    share = lax.dynamic_slice_in_dim(factors, column_index * half, half, 0)
+    own = lax.dynamic_slice_in_dim(factors, core * own_count, own_count, 0)
+    pieces = share.reshape(group_count, half * virt_width // group_count, naux_width)
+    mixed = lax.all_to_all(pieces, "occ", split_axis=0, concat_axis=0, tiled=True)
+    shape = (half, virt_width, naux_width)
+    first = jnp.take(mixed, pairing[0], axis=0)
+    near_0 = lax.all_to_all(first, "occ", split_axis=0, concat_axis=0, tiled=True).reshape(shape)
+    far_0 = lax.ppermute(near_0, "virt", twin)
+    mixed_late, _ = lax.optimization_barrier((mixed, near_0))
+    second = jnp.take(mixed_late, pairing[1], axis=0)
+    near_1 = exchange_pieces(second, group_index, group_count).reshape(shape)
+    far_1 = lax.ppermute(near_1, "virt", twin)
+
+    grouped = occ_energy.reshape(group_count, groups_rows)
+    own_energy = lax.dynamic_slice_in_dim(grouped[group_index], core * own_count, own_count, 0)
+
+    def energy_of_mates(round_index):
+        mate = grouped[pairing[round_index, group_index]]
+        near_part = lax.dynamic_slice_in_dim(mate, column_index * half, half, 0)
+        far_part = lax.dynamic_slice_in_dim(
+            mate, (place * CORES + 1 - core) * half, half, 0
+        )
+        return jnp.concatenate([near_part, far_part])
+
+    mates_0 = energy_of_mates(0)
+    carried, energy_0 = pair_rows(
+        own, 0, own_count, near_0, far_0, own_energy, mates_0, virt_energy, None
+    )
+    mates_1 = energy_of_mates(1)
+    sizes = [own_count - own_count // 2] + [1] * (own_count // 2)
+    start, energy_1, mine, theirs = 0, [], [], []
+    for rows in sizes:
+        grad, energy = pair_rows(
+            own, start, rows, near_1, far_1, own_energy, mates_1, virt_energy, carried
+        )
+        start += rows
+        energy_1.append(energy)
+        parts = grad.reshape(rows, span, CORES * slab, naux_width)
+        kept = lax.dynamic_index_in_dim(parts, place, 1, keepdims=False)
+        for shift in range(1, span):
+            sent = lax.dynamic_index_in_dim(parts, lax.rem(place + shift, span), 1, keepdims=False)
+            kept = kept + lax.ppermute(
+                sent,
+                "virt",
+                [(v, (v + shift * CORES) % virt_count) for v in range(virt_count)],
+            )
+        mine.append(lax.dynamic_slice_in_dim(kept, core * slab, slab, 1))
+        theirs.append(
+            lax.ppermute(
+                lax.dynamic_slice_in_dim(kept, (1 - core) * slab, slab, 1), "virt", twin
+            )
+        )
+    mine, theirs = jnp.concatenate(mine), jnp.concatenate(theirs)
+    gradient = jnp.where(
+        core == 0, jnp.concatenate([mine, theirs]), jnp.concatenate([theirs, mine])
+    )
+    energies = jnp.stack([energy_0, jnp.concatenate(energy_1)])
+    energies = energies / (virt_width * groups_rows * virt_width)
+    placed = lax.dynamic_update_slice_in_dim(
+        jnp.zeros((2, groups_rows), jnp.float32), energies, core * own_count, 1
+    )
+    return lax.psum(placed, "virt"), gradient
+
+
 def solution(mesh):
     placed = (P("occ", None, None), P(), P(), P())
+
     return jax.shard_map(
         per_device,
         mesh=mesh,

time: 523 us -> 306 us (0.59)
  the two profiles are of different devices: /device:TPU:0 before, /device:TPU:10 now
where the time goes in v2:
time: 306 us; the launch traced here: 305 us
  waiting for transfers between devices  126 us (41%)
  Pallas kernels  87.7 us (29%)
  starting transfers between devices  35.7 us (12%)
  local copies, waits for them, and re-layouts  26.2 us (9%)
  other arithmetic  17.4 us (6%)
  blocking collectives  6.91 us (2%)
  between operations  4.81 us (2%)
    pallas_call x4, Pallas kernels, pair_rows(): pl.pallas_call(functools.partial(pair_kernel, half), grid_spec=pltpu.Pref...  87.7 us
    all_to_all x1, waiting for transfers between devices, per_device(): lax.all_to_all(pieces, 'occ', split_axis=0, concat_axis=0, tiled=True)  44.9 us
    all_to_all x1, waiting for transfers between devices, per_device(): lax.all_to_all(first, 'occ', split_axis=0, concat_axis=0, tiled=True)  38.5 us
    ppermute x7, waiting for transfers between devices, exchange_pieces(): lax.ppermute(sent, 'occ', [(s, (s + shift) % group_count) for s in range(...  31.4 us
    ppermute x7, starting transfers between devices, exchange_pieces(): lax.ppermute(sent, 'occ', [(s, (s + shift) % group_count) for s in range(...  17.3 us
    ppermute x3, waiting for transfers between devices, per_device(): lax.ppermute(sent, 'virt', [(v, (v + shift * CORES) % virt_count) for v i...  11.4 us
    all_to_all x1, starting transfers between devices, per_device(): lax.all_to_all(first, 'occ', split_axis=0, concat_axis=0, tiled=True)  7.67 us
    psum x1, blocking collectives, per_device(): return (lax.psum(placed, 'virt'), gradient)  6.91 us
  transfers between devices with their start and end apart: 17, of which 8 were waited for; matrix products, arithmetic and copies ran while one was open for 10% of the time, Pallas kernels for 24%

profile of v2, /device:TPU:10, one launch (start us, length us, event | category | flops | bytes accessed | tf_op | source)
XLA Modules:
  0.0 305.0 jit_solution(8292939734560926397)
XLA Ops:
  0.6 3.1 %constant_dynamic-slice_fusion.10 = f32[2,512,512]{2,1,0:T(8,128)} fusion(f32[8,512,512]{2,1,0:T(8,128)} %param.6, s32[]{:T(128)S(6)} %select_n.124), kind=kLoop, calls=%fused_computation.41 | loop fusion | bytes 4194308 | tf_op jit(solution)/shard_map/dynamic_slice | solution.py:281
  3.7 6.4 %all-to-all-start = ((f32[8,128,512]{2,1,0:T(8,128)}), f32[8,128,512]{2,1,0:T(8,128)S(1)}, u32[]{:S(2)}, u32[]{:S(2)}) async-start(f32[8,128,512]{2,1,0:T(8,128)} %bitcast.55), calls=%async_computation | async-start | bytes 4194304 | tf_op jit(solution)/shard_map/all_to_all | solution.py:284
  10.1 44.9 %all-to-all-done = f32[8,128,512]{2,1,0:T(8,128)S(1)} async-done(((f32[8,128,512]{2,1,0:T(8,128)}), f32[8,128,512]{2,1,0:T(8,128)S(1)}, u32[]{:S(2)}, u32[]{:S(2)}) %all-to-all-start) | async-done | bytes 2097184 | tf_op jit(solution)/shard_map/all_to_all | solution.py:284
  55.0 2.0 gather_fusion
  57.0 3.3 %broadcast_select_fusion.1 = f32[8,128,512]{2,1,0:T(8,128)} fusion(f32[8,128,512]{2,1,0:T(8,128)} %gather_fusion, pred[8]{0:T(512)(128)(4,1)S(1)} %get-tuple-element.45), kind=kLoop, calls=%fused_computation.4 | loop fusion | flops 524288 | bytes 4194312 | tf_op jit(solution)/shard_map/jit(_take)/select_n | solution.py:286
  60.3 7.7 %all-to-all-start.1 = ((f32[8,128,512]{2,1,0:T(8,128)}), f32[8,128,512]{2,1,0:T(8,128)}, u32[]{:S(2)}, u32[]{:S(2)}) async-start(f32[8,128,512]{2,1,0:T(8,128)} %broadcast_select_fusion.1), calls=%async_computation.1 | async-start | bytes 4194304 | tf_op jit(solution)/shard_map/all_to_all | solution.py:287
  72.6 0.6 fusion
  73.3 0.6 pad_bitcast_fusion.1
  74.0 38.5 %all-to-all-done.1 = f32[8,128,512]{2,1,0:T(8,128)} async-done(((f32[8,128,512]{2,1,0:T(8,128)}), f32[8,128,512]{2,1,0:T(8,128)}, u32[]{:S(2)}, u32[]{:S(2)}) %all-to-all-start.1) | async-done | bytes 2097184 | tf_op jit(solution)/shard_map/all_to_all | solution.py:287
  112.5 0.7 maximum_bitcast_fusion.1
  113.3 4.6 %constant_dynamic-slice_fusion.11.own_ref = f32[4,512,512]{2,1,0:T(8,128)} fusion(f32[8,512,512]{2,1,0:T(8,128)} %param.6, s32[]{:T(128)S(6)} %select_n.120), kind=kLoop, calls=%fused_computation.42 | loop fusion | bytes 8388612 | tf_op jit(solution)/shard_map/dynamic_slice | solution.py:282
  117.8 2.0 gather_fusion.1
  119.8 1.9 broadcast_select_fusion
  122.0 1.0 constant_dynamic-slice_fusion.3
  123.0 1.5 collective-permute-start.1
  125.1 3.3 %collective-permute-start.2 = (f32[1,128,512]{2,1,0:T(8,128)}, f32[1,128,512]{2,1,0:T(8,128)}, u32[]{:S(2)}, u32[]{:S(2)}) collective-permute-start(f32[1,128,512]{2,1,0:T(8,128)} %get-tuple-element.30), channel_id=1, source_target_pairs={{0,8},{4,12},{8,16},{12,20},{16,24},{20,28},{24,0},{28,4},{1,9},{5... | collective-permute-start | bytes 786440 | tf_op jit(solution)/shard_map/ppermute | solution.py:258
  128.4 2.5 collective-permute-start.3
  131.5 0.9 copy.6.left_ref
  132.3 6.4 %collective-permute-start.5 = (f32[1,128,512]{2,1,0:T(8,128)S(1)}, f32[1,128,512]{2,1,0:T(8,128)S(1)}, u32[]{:S(2)}, u32[]{:S(2)}) collective-permute-start(f32[1,128,512]{2,1,0:T(8,128)S(1)} %get-tuple-element.27), channel_id=1, source_target_pairs={{0,20},{4,24},{8,28},{12,0},{16,4},{20,8},{24,12},{28,16},{1,21},{... | collective-permute-start | bytes 786440 | tf_op jit(solution)/shard_map/ppermute | solution.py:258
  138.7 1.0 constant_dynamic-update-slice_fusion.12
  139.7 3.8 %collective-permute-start.6 = (f32[1,128,512]{2,1,0:T(8,128)S(1)}, f32[1,128,512]{2,1,0:T(8,128)S(1)}, u32[]{:S(2)}, u32[]{:S(2)}) collective-permute-start(f32[1,128,512]{2,1,0:T(8,128)S(1)} %get-tuple-element.26), channel_id=1, source_target_pairs={{0,24},{4,28},{8,0},{12,4},{16,8},{20,12},{24,16},{28,20},{1,25},{... | collective-permute-start | bytes 786440 | tf_op jit(solution)/shard_map/ppermute | solution.py:258
  143.4 1.0 constant_dynamic-update-slice_fusion.11
  144.4 20.7 %collective-permute-done.3 = f32[1,128,512]{2,1,0:T(8,128)} collective-permute-done((f32[1,128,512]{2,1,0:T(8,128)S(1)}, f32[1,128,512]{2,1,0:T(8,128)}, u32[]{:S(2)}, u32[]{:S(2)}) %collective-permute-start.3) | collective-permute-done | bytes 262176 | tf_op jit(solution)/shard_map/ppermute | solution.py:258
  165.1 1.0 constant_dynamic-update-slice_fusion.10
  166.1 4.2 %collective-permute-done.4 = f32[1,128,512]{2,1,0:T(8,128)S(1)} collective-permute-done((f32[1,128,512]{2,1,0:T(8,128)S(1)}, f32[1,128,512]{2,1,0:T(8,128)S(1)}, u32[]{:S(2)}, u32[]{:S(2)}) %collective-permute-start.4) | collective-permute-done | bytes 262176 | tf_op jit(solution)/shard_map/ppermute | solution.py:258
  170.3 4.7 %collective-permute-done.6 = f32[1,128,512]{2,1,0:T(8,128)S(1)} collective-permute-done((f32[1,128,512]{2,1,0:T(8,128)S(1)}, f32[1,128,512]{2,1,0:T(8,128)S(1)}, u32[]{:S(2)}, u32[]{:S(2)}) %collective-permute-start.6) | collective-permute-done | bytes 262176 | tf_op jit(solution)/shard_map/ppermute | solution.py:258
  175.1 1.8 collective-permute-done.7
  177.0 38.9 %pair_rows.4 = (f32[4,512,512]{2,1,0:T(8,128)}, f32[4,4,8,512]{3,2,1,0:T(8,128)}) custom-call(f32[2,4]{1,0:T(2,128)} %pad_maximum_fusion.3.energies_ref, f32[4,512,512]{2,1,0:T(8,128)} %constant_dynamic-slice_fusion.11.own_ref, f32[2,512,512]{2,1,0:T(8,128)} %bitcast.6.near_ref, f32[2,512,512]{2,1,0:T(8,128)} %collective-permute-done.far_ref, ...), custom_call_target="tpu_custom_call" | custom-call | flops 25769803776 | bytes 16777216 | tf_op jit(solution)/shard_map/pair_rows/pallas_call | solution.py:224
  215.9 1.1 reduce_sum.40
  216.9 13.3 %pair_rows.6 = (f32[1,512,512]{2,1,0:T(8,128)}, f32[1,4,8,512]{3,2,1,0:T(8,128)}) custom-call(f32[2,4]{1,0:T(2,128)} %get-tuple-element.48.energies_ref, f32[4,512,512]{2,1,0:T(8,128)} %constant_dynamic-slice_fusion.11.own_ref, f32[2,512,512]{2,1,0:T(8,128)} %bitcast.59, f32[2,512,512]{2,1,0:T(8,128)} %collective-permute-done.8.far_ref, ...), custom_call_target="tpu_custom_call" | custom-call | flops 6442450944 | bytes 16777216 | tf_op jit(solution)/shard_map/pair_rows/pallas_call | solution.py:224
  230.2 1.9 dynamic-slice_bitcast_fusion.2
  232.1 1.5 collective-permute-start.10
  233.6 22.1 %pair_rows.5 = (f32[2,512,512]{2,1,0:T(8,128)}, f32[2,4,8,512]{3,2,1,0:T(8,128)}) custom-call(f32[2,4]{1,0:T(2,128)} %get-tuple-element.47.energies_ref, f32[4,512,512]{2,1,0:T(8,128)} %constant_dynamic-slice_fusion.11.own_ref, f32[2,512,512]{2,1,0:T(8,128)} %bitcast.60, f32[2,512,512]{2,1,0:T(8,128)} %collective-permute-done.8.far_ref, ...), custom_call_target="tpu_custom_call" | custom-call | flops 12884901888 | bytes 16777216 | tf_op jit(solution)/shard_map/pair_rows/pallas_call | solution.py:224
  255.8 1.3 dynamic-slice_bitcast_fusion
  257.6 13.4 %pair_rows.7 = (f32[1,512,512]{2,1,0:T(8,128)}, f32[1,4,8,512]{3,2,1,0:T(8,128)}) custom-call(f32[2,4]{1,0:T(2,128)} %get-tuple-element.49.energies_ref, f32[4,512,512]{2,1,0:T(8,128)} %constant_dynamic-slice_fusion.11.own_ref, f32[2,512,512]{2,1,0:T(8,128)} %bitcast.61, f32[2,512,512]{2,1,0:T(8,128)} %collective-permute-done.8.far_ref, ...), custom_call_target="tpu_custom_call" | custom-call | flops 6442450944 | bytes 16777216 | tf_op jit(solution)/shard_map/pair_rows/pallas_call | solution.py:224
  271.0 2.0 dynamic-slice_bitcast_fusion.1
  273.0 1.5 collective-permute-start.11
  275.3 1.5 reduce_sum.44
  276.8 1.4 maximum_bitcast_fusion.2
  278.1 1.3 bitcast_add_fusion.2
  279.4 3.8 %collective-permute-done.9 = f32[2,256,512]{2,1,0:T(8,128)} collective-permute-done((f32[2,256,512]{2,1,0:T(8,128)S(1)}, f32[2,256,512]{2,1,0:T(8,128)}, u32[]{:S(2)}, u32[]{:S(2)}) %collective-permute-start.9) | collective-permute-done | bytes 1048608 | tf_op jit(solution)/shard_map/ppermute | solution.py:322
  283.3 1.4 bitcast_add_fusion
  284.7 0.8 constant_dynamic-slice_fusion.2
  286.1 7.6 %collective-permute-done.11 = f32[1,256,512]{2,1,0:T(8,128)} collective-permute-done((f32[1,256,512]{2,1,0:T(8,128)}, f32[1,256,512]{2,1,0:T(8,128)}, u32[]{:S(2)}, u32[]{:S(2)}) %collective-permute-start.11) | collective-permute-done | bytes 524320 | tf_op jit(solution)/shard_map/ppermute | solution.py:322
  293.7 1.1 bitcast_add_fusion.1
  294.9 0.7 constant_dynamic-slice_fusion
  295.8 6.9 %psum.7 = f32[2,8]{1,0:T(2,128)} all-reduce(f32[2,8]{1,0:T(2,128)S(1)} %dynamic_update_slice.36), channel_id=1, replica_groups=mesh['occ'=8,'virt'=4] {'virt'}, use_global_device_ids=true, to_apply=%region_4.6 | all-reduce | flops 16 | bytes 128 | tf_op jit(solution)/shard_map/psum | solution.py:342
  303.2 1.8 broadcast_select_fusion.2
  (68 shorter events, 5.1 us)
Async XLA Ops:
  3.7 6.4 %copy-start.7 = (s32[2,8]{1,0:T(2,128)S(1)}, s32[2,8]{1,0:T(2,128)}, u32[]{:S(2)}) copy-start(s32[2,8]{1,0:T(2,128)} %param.9) | copy-start | bytes 196
  3.7 51.3 %all-to-all-start = ((f32[8,128,512]{2,1,0:T(8,128)}), f32[8,128,512]{2,1,0:T(8,128)S(1)}, u32[]{:S(2)}, u32[]{:S(2)}) async-start(f32[8,128,512]{2,1,0:T(8,128)} %bitcast.55), calls=%async_computation | async-start | bytes 4194304 | tf_op jit(solution)/shard_map/all_to_all | solution.py:284
  60.3 12.1 %copy-start.9 = (f32[64]{0:T(128)S(1)}, f32[64]{0:T(128)}, u32[]{:S(2)}) copy-start(f32[64]{0:T(128)} %param.7) | copy-start | bytes 772
  60.3 52.2 %all-to-all-start.1 = ((f32[8,128,512]{2,1,0:T(8,128)}), f32[8,128,512]{2,1,0:T(8,128)}, u32[]{:S(2)}, u32[]{:S(2)}) async-start(f32[8,128,512]{2,1,0:T(8,128)} %broadcast_select_fusion.1), calls=%async_computation.1 | async-start | bytes 4194304 | tf_op jit(solution)/shard_map/all_to_all | solution.py:287
  112.5 64.4 %collective-permute-start = (f32[2,512,512]{2,1,0:T(8,128)}, f32[2,512,512]{2,1,0:T(8,128)}, u32[]{:S(2)}, u32[]{:S(2)}) collective-permute-start(f32[2,512,512]{2,1,0:T(8,128)} %bitcast.6.near_ref), channel_id=1, source_target_pairs={{0,1},{1,0},{2,3},{3,2},{4,5},{5,4},{6,7},{7,6},{8,9},{9,8},{10,11... | collective-permute-start | bytes 6291464 | tf_op jit(solution)/shard_map/ppermute | solution.py:288
  122.0 9.5 %copy-start.8 = (f32[512]{0:T(512)S(1)}, f32[512]{0:T(512)}, u32[]{:S(2)}) copy-start(f32[512]{0:T(512)} %param.8) | copy-start | bytes 6148
  123.0 9.3 %collective-permute-start.1 = (f32[1,128,512]{2,1,0:T(8,128)}, f32[1,128,512]{2,1,0:T(8,128)}, u32[]{:S(2)}, u32[]{:S(2)}) collective-permute-start(f32[1,128,512]{2,1,0:T(8,128)} %get-tuple-element.31), channel_id=1, source_target_pairs={{0,4},{4,8},{8,12},{12,16},{16,20},{20,24},{24,28},{28,0},{1,5},{5... | collective-permute-start | bytes 786440 | tf_op jit(solution)/shard_map/ppermute | solution.py:258
  125.1 14.6 %collective-permute-start.2 = (f32[1,128,512]{2,1,0:T(8,128)}, f32[1,128,512]{2,1,0:T(8,128)}, u32[]{:S(2)}, u32[]{:S(2)}) collective-permute-start(f32[1,128,512]{2,1,0:T(8,128)} %get-tuple-element.30), channel_id=1, source_target_pairs={{0,8},{4,12},{8,16},{12,20},{16,24},{20,28},{24,0},{28,4},{1,9},{5... | collective-permute-start | bytes 786440 | tf_op jit(solution)/shard_map/ppermute | solution.py:258
  128.4 36.7 %collective-permute-start.3 = (f32[1,128,512]{2,1,0:T(8,128)S(1)}, f32[1,128,512]{2,1,0:T(8,128)}, u32[]{:S(2)}, u32[]{:S(2)}) collective-permute-start(f32[1,128,512]{2,1,0:T(8,128)S(1)} %get-tuple-element.29), channel_id=1, source_target_pairs={{0,12},{4,16},{8,20},{12,24},{16,28},{20,0},{24,4},{28,8},{1,13},{... | collective-permute-start | bytes 786440 | tf_op jit(solution)/shard_map/ppermute | solution.py:258
  132.3 38.0 %collective-permute-start.4 = (f32[1,128,512]{2,1,0:T(8,128)S(1)}, f32[1,128,512]{2,1,0:T(8,128)S(1)}, u32[]{:S(2)}, u32[]{:S(2)}) collective-permute-start(f32[1,128,512]{2,1,0:T(8,128)S(1)} %get-tuple-element.28), channel_id=1, source_target_pairs={{0,16},{4,20},{8,24},{12,28},{16,0},{20,4},{24,8},{28,12},{1,17},{... | collective-permute-start | bytes 786440 | tf_op jit(solution)/shard_map/ppermute | solution.py:258
  132.3 38.0 %collective-permute-start.5 = (f32[1,128,512]{2,1,0:T(8,128)S(1)}, f32[1,128,512]{2,1,0:T(8,128)S(1)}, u32[]{:S(2)}, u32[]{:S(2)}) collective-permute-start(f32[1,128,512]{2,1,0:T(8,128)S(1)} %get-tuple-element.27), channel_id=1, source_target_pairs={{0,20},{4,24},{8,28},{12,0},{16,4},{20,8},{24,12},{28,16},{1,21},{... | collective-permute-start | bytes 786440 | tf_op jit(solution)/shard_map/ppermute | solution.py:258
  139.7 35.4 %collective-permute-start.6 = (f32[1,128,512]{2,1,0:T(8,128)S(1)}, f32[1,128,512]{2,1,0:T(8,128)S(1)}, u32[]{:S(2)}, u32[]{:S(2)}) collective-permute-start(f32[1,128,512]{2,1,0:T(8,128)S(1)} %get-tuple-element.26), channel_id=1, source_target_pairs={{0,24},{4,28},{8,0},{12,4},{16,8},{20,12},{24,16},{28,20},{1,25},{... | collective-permute-start | bytes 786440 | tf_op jit(solution)/shard_map/ppermute | solution.py:258
  165.1 11.7 %collective-permute-start.7 = (f32[1,128,512]{2,1,0:T(8,128)S(1)}, f32[1,128,512]{2,1,0:T(8,128)S(1)}, u32[]{:S(2)}, u32[]{:S(2)}) collective-permute-start(f32[1,128,512]{2,1,0:T(8,128)S(1)} %get-tuple-element.25), channel_id=1, source_target_pairs={{0,28},{4,0},{8,4},{12,8},{16,12},{20,16},{24,20},{28,24},{1,29},{... | collective-permute-start | bytes 786440 | tf_op jit(solution)/shard_map/ppermute | solution.py:258
  176.9 39.0 %copy-start.1 = (f32[8,128,512]{2,1,0:T(8,128)}, f32[8,128,512]{2,1,0:T(8,128)S(1)}, u32[]{:S(2)}) copy-start(f32[8,128,512]{2,1,0:T(8,128)S(1)} %constant_dynamic-update-slice_fusion.6) | copy-start | bytes 6291460
  176.9 40.1 %collective-permute-start.8 = (f32[2,512,512]{2,1,0:T(8,128)S(1)}, f32[2,512,512]{2,1,0:T(8,128)}, u32[]{:S(2)}, u32[]{:S(2)}) collective-permute-start(f32[2,512,512]{2,1,0:T(8,128)S(1)} %bitcast.58), channel_id=1, source_target_pairs={{0,1},{1,0},{2,3},{3,2},{4,5},{5,4},{6,7},{7,6},{8,9},{9,8},{10,11... | collective-permute-start | bytes 6291464 | tf_op jit(solution)/shard_map/ppermute | solution.py:292
  232.1 46.0 %collective-permute-start.10 = (f32[1,256,512]{2,1,0:T(8,128)}, f32[1,256,512]{2,1,0:T(8,128)}, u32[]{:S(2)}, u32[]{:S(2)}) collective-permute-start(f32[1,256,512]{2,1,0:T(8,128)} %dynamic-slice_bitcast_fusion.2), channel_id=1, source_target_pairs={{0,2},{1,3},{2,0},{3,1},{4,6},{5,7},{6,4},{7,5},{8,10},{9,11},{10,... | collective-permute-start | bytes 1572872 | tf_op jit(solution)/shard_map/ppermute | solution.py:322
  257.1 26.2 %collective-permute-start.9 = (f32[2,256,512]{2,1,0:T(8,128)S(1)}, f32[2,256,512]{2,1,0:T(8,128)}, u32[]{:S(2)}, u32[]{:S(2)}) collective-permute-start(f32[2,256,512]{2,1,0:T(8,128)S(1)} %dynamic-slice_bitcast_fusion), channel_id=1, source_target_pairs={{0,2},{1,3},{2,0},{3,1},{4,6},{5,7},{6,4},{7,5},{8,10},{9,11},{10,... | collective-permute-start | bytes 3145736 | tf_op jit(solution)/shard_map/ppermute | solution.py:322
  257.6 16.9 %copy-start.5 = (f32[2,4,8,512]{3,2,1,0:T(8,128)S(1)}, f32[2,4,8,512]{3,2,1,0:T(8,128)}, u32[]{:S(2)}) copy-start(f32[2,4,8,512]{3,2,1,0:T(8,128)} %get-tuple-element.15) | copy-start | bytes 393220
  257.6 17.1 %copy-start.6 = (f32[1,4,8,512]{3,2,1,0:T(8,128)S(1)}, f32[1,4,8,512]{3,2,1,0:T(8,128)}, u32[]{:S(2)}) copy-start(f32[1,4,8,512]{3,2,1,0:T(8,128)} %get-tuple-element.16) | copy-start | bytes 196612
  271.0 12.3 %copy-start = (f32[2,512,512]{2,1,0:T(8,128)S(1)}, f32[2,512,512]{2,1,0:T(8,128)}, u32[]{:S(2)}) copy-start(f32[2,512,512]{2,1,0:T(8,128)} %get-tuple-element.18) | copy-start | bytes 6291460
  273.0 20.7 %collective-permute-start.11 = (f32[1,256,512]{2,1,0:T(8,128)}, f32[1,256,512]{2,1,0:T(8,128)}, u32[]{:S(2)}, u32[]{:S(2)}) collective-permute-start(f32[1,256,512]{2,1,0:T(8,128)} %dynamic-slice_bitcast_fusion.1), channel_id=1, source_target_pairs={{0,2},{1,3},{2,0},{3,1},{4,6},{5,7},{6,4},{7,5},{8,10},{9,11},{10,... | collective-permute-start | bytes 1572872 | tf_op jit(solution)/shard_map/ppermute | solution.py:322
  279.4 6.1 %copy-start.2 = (f32[1,256,512]{2,1,0:T(8,128)}, f32[1,256,512]{2,1,0:T(8,128)S(1)}, u32[]{:S(2)}) copy-start(f32[1,256,512]{2,1,0:T(8,128)S(1)} %bitcast_add_fusion.2) | copy-start | bytes 1572868
  279.4 14.3 %copy-start.4 = (f32[1,512,512]{2,1,0:T(8,128)S(1)}, f32[1,512,512]{2,1,0:T(8,128)}, u32[]{:S(2)}) copy-start(f32[1,512,512]{2,1,0:T(8,128)} %get-tuple-element.20) | copy-start | bytes 3145732
  285.5 17.1 %collective-permute-start.12 = (f32[2,128,512]{2,1,0:T(8,128)}, f32[2,128,512]{2,1,0:T(8,128)S(1)}, u32[]{:S(2)}, u32[]{:S(2)}) collective-permute-start(f32[2,128,512]{2,1,0:T(8,128)} %constant_dynamic-slice_fusion.2), channel_id=1, source_target_pairs={{0,1},{1,0},{2,3},{3,2},{4,5},{5,4},{6,7},{7,6},{8,9},{9,8},{10,11... | collective-permute-start | bytes 1572872 | tf_op jit(solution)/shard_map/ppermute | solution.py:329
  285.6 17.1 %collective-permute-start.13 = (f32[1,128,512]{2,1,0:T(8,128)S(1)}, f32[1,128,512]{2,1,0:T(8,128)S(1)}, u32[]{:S(2)}, u32[]{:S(2)}) collective-permute-start(f32[1,128,512]{2,1,0:T(8,128)S(1)} %constant_dynamic-slice_fusion.1), channel_id=1, source_target_pairs={{0,1},{1,0},{2,3},{3,2},{4,5},{5,4},{6,7},{7,6},{8,9},{9,8},{10,11... | collective-permute-start | bytes 786440 | tf_op jit(solution)/shard_map/ppermute | solution.py:329
  294.8 8.1 %copy-start.3 = (f32[1,256,512]{2,1,0:T(8,128)S(1)}, f32[1,256,512]{2,1,0:T(8,128)}, u32[]{:S(2)}) copy-start(f32[1,256,512]{2,1,0:T(8,128)} %copy-done.2) | copy-start | bytes 1572868
  295.6 7.2 %collective-permute-start.14 = (f32[1,128,512]{2,1,0:T(8,128)}, f32[1,128,512]{2,1,0:T(8,128)S(1)}, u32[]{:S(2)}, u32[]{:S(2)}) collective-permute-start(f32[1,128,512]{2,1,0:T(8,128)} %constant_dynamic-slice_fusion), channel_id=1, source_target_pairs={{0,1},{1,0},{2,3},{3,2},{4,5},{5,4},{6,7},{7,6},{8,9},{9,8},{10,11... | collective-permute-start | bytes 786440 | tf_op jit(solution)/shard_map/ppermute | solution.py:329
